TPU v7x, 256 devices: a whole 4x4x8 slice. The times are simulated.
256 devices in a mesh: dp: 32 (over z, y_lo, core), tensor: 8 (over x, y_hi).
Axes of the slice: x: 4, y: 4 (y_hi: 2, y_lo: 2; y = y_hi * 2 + y_lo), z: 8, core: 2. Of those that a mesh axis runs over, the one named last changes fastest.
Arguments:
- projected: bfloat16 [3, 16384, 2560], P(None, 'dp', 'tensor'), may hold values from -40 to 40
- residue_counts: int32 [32], P('dp'), may hold values from 64 to 512, as said below
- migrate_plan: int32 [32], P('dp'), may hold values from 0 to 1, as said below
- out_weight: bfloat16 [2560, 2560], P('tensor', 'dp'), may hold values from -0.125 to 0.125
- out_cotangent: bfloat16 [64, 512, 2560], P('dp', None, 'tensor'), may hold values from -6 to 6
Outputs:
- layer_out: bfloat16 [64, 512, 2560], P('dp', None, 'tensor')
- grad_projected: bfloat16 [3, 16384, 2560], P(None, 'dp', 'tensor')
- grad_weight: float32 [2560, 2560], P('tensor', 'dp')
Inputs may be any that keep to these rules, and one draw needn't show every extreme that they name: `residue_counts`: some tile has all 512 positions real, and some has exactly 64. migrate_plan[o] = 1 exactly where the sum of residue_counts over the 1 tiles of o exceeds that of its partner (o + 16) % 32 by more than 128, else 0; so never both devices of a pair have 1.
All inputs are finite; a program needn't handle non-finite values.
Results may differ from a plain program's by a relative error of at most 0.02.
Values may be sent and summed in bfloat16 or wider, within the bound.
No kernel may reach another device: no remote copies, remote signals or barrier semaphores. Data moves between devices by JAX's collectives and lax.ppermute only.
A program may use at most 128 MiB of HBM per device.

v0:
```python
import jax
import jax.numpy as jnp
from jax import lax
from jax.sharding import PartitionSpec as P

HEAD_DIM = 64


def shifted(shard, axis, by):
    peers = lax.axis_size(axis)
    return lax.ppermute(shard, axis, [(i, (i + by) % peers) for i in range(peers)])


def attend(tile_qkv, count):
    length = tile_qkv.shape[1]
    columns = tile_qkv.shape[2]
    head_count = columns // HEAD_DIM
    queries = tile_qkv[0].reshape(length, head_count, HEAD_DIM)
    key_rows = tile_qkv[1].reshape(length, head_count, HEAD_DIM)
    values = tile_qkv[2].reshape(length, head_count, HEAD_DIM)
    scores = jnp.einsum(
        "qhd,khd->hqk", queries, key_rows, preferred_element_type=jnp.float32
    ) * HEAD_DIM ** (-0.5)
    position = lax.iota(jnp.int32, length)
    live_mask = position < count
    scores = jnp.where(live_mask[None, None, :], scores, -1000000000.0)
    row_max = jnp.max(scores, axis=2, keepdims=True)
    exponent = jnp.exp(scores - row_max)
    weights = (exponent / jnp.sum(exponent, axis=2, keepdims=True)).astype(jnp.bfloat16)
    context = jnp.einsum("hqk,khd->qhd", weights, values, preferred_element_type=jnp.float32)
    context = context * live_mask.astype(jnp.float32)[:, None, None]
    return context.reshape(length, columns)


def tile_grad(tile_qkv, count, tile_cot):
    _, pullback = jax.vjp(lambda operand: attend(operand, count), tile_qkv)
    return pullback(tile_cot.astype(jnp.float32))[0]


def shards(projected, residue_counts, migrate_plan, out_weight, out_cotangent):
    home_tiles = residue_counts.shape[0]
    length = projected.shape[1] // home_tiles
    columns = projected.shape[2]
    half_axis = lax.axis_size("dp") // 2
    home_qkv = projected.reshape(3, home_tiles, length, columns)
    sent_flag = migrate_plan[0]
    guest_meta = jnp.stack([residue_counts[home_tiles - 1] * sent_flag, sent_flag])
    guest_tile, guest_info = shifted((home_qkv[:, home_tiles - 1], guest_meta), "dp", half_axis)
    slot_qkv = jnp.concatenate([home_qkv, guest_tile[:, None]], axis=1)
    keep_last = residue_counts[home_tiles - 1] * (1 - sent_flag)
    live_counts = jnp.concatenate(
        [residue_counts[: home_tiles - 1], keep_last[None], guest_info[0:1]]
    ).astype(jnp.int32)
    context = jax.vmap(attend, in_axes=(1, 0))(slot_qkv, live_counts).astype(jnp.bfloat16)
    row_count = context.shape[0] * length
    flat_ctx = context.reshape(row_count, columns)
    whole_weight = lax.all_gather(out_weight, "dp", axis=1, tiled=True)
    partial_value = jnp.dot(flat_ctx, whole_weight, preferred_element_type=jnp.float32)
    summed = lax.psum_scatter(
        partial_value.astype(jnp.bfloat16), "tensor", scatter_dimension=1, tiled=True
    )
    layer_out = summed.reshape(home_tiles + 1, length, -1)
    full_cot = lax.all_gather(out_cotangent, "tensor", axis=2, tiled=True).reshape(row_count, -1)
    contract_cols = (((1,), (1,)), ((), ()))
    grad_context = lax.dot_general(
        full_cot, whole_weight, contract_cols, preferred_element_type=jnp.float32
    )
    grad_context = grad_context.astype(jnp.bfloat16).reshape(home_tiles + 1, length, columns)
    weight_term = lax.dot_general(
        flat_ctx, full_cot, (((0,), (0,)), ((), ())), preferred_element_type=jnp.float32
    )
    grad_weight = lax.psum_scatter(
        weight_term.astype(jnp.bfloat16), "dp", scatter_dimension=1, tiled=True
    ).astype(jnp.float32)
    slot_grads = jax.vmap(tile_grad, in_axes=(1, 0, 0), out_axes=1)(
        slot_qkv, live_counts, grad_context
    )
    returned = shifted(slot_grads[:, home_tiles], "dp", half_axis)
    last_grad = jnp.where(sent_flag > 0, returned, slot_grads[:, home_tiles - 1])
    home_grads = jnp.concatenate([slot_grads[:, : home_tiles - 1], last_grad[:, None]], axis=1)
    grad_projected = home_grads.reshape(3, home_tiles * length, columns)
    return (layer_out, grad_projected, grad_weight)


def solution(mesh):
    in_specs = (
        P(None, "dp", "tensor"),
        P("dp"),
        P("dp"),
        P("tensor", "dp"),
        P("dp", None, "tensor"),
    )
    out_specs = (P("dp", None, "tensor"), P(None, "dp", "tensor"), P("tensor", "dp"))
    return jax.shard_map(shards, mesh=mesh, in_specs=in_specs, out_specs=out_specs, check_vma=False)
```

profile of v0, /device:TPU:1, one launch (start us, length us, event | category | flops | bytes accessed | tf_op | source)
XLA Modules:
  0.0 443.2 jit_solution(11317257145265913839)
XLA Ops:
  7.2 0.0 all-gather.5.cloned.1.call-start
  7.2 0.7 all-gather.5.cloned.1.call-update
  7.9 0.0 all-gather.3.cloned.1.call-start
  7.9 0.7 all-gather.3.cloned.1.call-update
  8.6 0.0 reduce-scatter.5.cloned.1.call-start
  8.7 7.8 %collective-permute-start = (bf16[3,512,320]{1,2,0:T(8,128)(2,1)}, bf16[3,512,320]{1,2,0:T(8,128)(2,1)S(1)}, u32[]{:S(2)}, u32[]{:S(2)}) collective-permute-start(bf16[3,512,320]{1,2,0:T(8,128)(2,1)} %param.5), channel_id=1, source_target_pairs={{0,128},{8,136},{16,144},{24,152},{32,160},{40,168},{48,176},{56,1... | collective-permute-start | bytes 2949128 | tf_op jit(solution)/shard_map/ppermute | solution.py:11
  17.8 0.1 pad_add_fusion
  17.9 0.0 collective-permute-start.1
  17.9 24.5 %collective-permute-done.1 = s32[2]{0:T(128)S(1)} collective-permute-done((s32[2]{0:T(128)S(1)}, s32[2]{0:T(128)S(1)}, u32[]{:S(2)}, u32[]{:S(2)}) %collective-permute-start.1) | collective-permute-done | bytes 40 | tf_op jit(solution)/shard_map/ppermute | solution.py:11
  42.4 0.1 pad_add_fusion.1
  42.5 0.1 fusion.33
  42.6 0.0 collective-permute-done
  42.6 1.3 pad_maximum_fusion
  43.9 0.0 copy-start.6
  43.9 0.0 copy-start.2
  44.0 2.5 fusion.5
  46.5 2.4 fusion.17
  49.0 1.6 copy-done
  50.6 48.2 %all-gather.5.cloned.1.call-done = bf16[2,512,2560]{1,2,0:T(8,128)(2,1)} async-done(((bf16[2,512,320]{1,2,0:T(8,128)(2,1)}), bf16[2,512,2560]{1,2,0:T(8,128)(2,1)}) %all-gather.5.cloned.1.call-update) | async-done | bytes 5242896 | tf_op jit(solution)/shard_map/all_gather | solution.py:63
  98.7 8.0 %copy.19 = bf16[2,512,2560]{2,1,0:T(8,128)(2,1)} copy(bf16[2,512,2560]{1,2,0:T(8,128)(2,1)} %all-gather.5.cloned.1.call-done) | data formatting | bytes 10485760 | tf_op jit(solution)/shard_map/all_gather | solution.py:63
  106.7 57.2 %all-gather.3.cloned.1.call-done = bf16[320,2560]{0,1:T(8,128)(2,1)} async-done(((bf16[320,80]{0,1:T(8,128)(2,1)}), bf16[320,2560]{0,1:T(8,128)(2,1)}) %all-gather.3.cloned.1.call-update) | async-done | bytes 1638416 | tf_op jit(solution)/shard_map/all_gather | solution.py:57
  163.9 6.1 %fusion.21 = f32[1024,320]{0,1:T(8,128)} fusion(bf16[1024,2560]{1,0:T(8,128)(2,1)} %bitcast.84, bf16[320,2560]{0,1:T(8,128)(2,1)} %all-gather.3.cloned.1.call-done), kind=kOutput, calls=%fused_computation.39 | convolution fusion | flops 1678376960 | bytes 8192000 | tf_op jit(solution)/shard_map/dot_general | solution.py:65
  170.1 2.5 reshape.93
  172.6 10.9 %convert_reduce_fusion = (f32[2,5,512]{2,1,0:T(8,128)S(1)}, pred[2,5,512,512]{2,3,1,0:T(32,128)(4,1)}, f32[2,5,512]{2,1,0:T(8,128)S(1)}, bf16[2,5,512,512]{2,3,1,0:T(8,128)(2,1)S(1)}) fusion(f32[2,5,512]{2,1,0:T(8,128)S(1)} %get-tuple-element.20, f32[2,5,512,512]{2,3,1,0:T(8,128)} %copy-done, pred[2,512]{1,0:T(4,128)(4,1)S(1)} %get-tuple-element.19, ...), kind=kOutput, calls=%fused_computation.7 | convolution fusion | flops 364697600 | bytes 20403200 | tf_op jit(solution)/shard_map/vmap(transpose(jvp(hqk,khd->qhd)))/dot_general | solution.py:30
  183.6 0.0 copy-start.3
  183.6 6.4 %fusion.34 = (f32[2,5,512]{2,1,0:T(8,128)S(1)}, f32[2,5,512,512]{2,3,1,0:T(8,128)}, bf16[2,5,512,512]{2,3,1,0:T(8,128)(2,1)S(1)}) fusion(f32[2,5,512]{2,1,0:T(8,128)S(1)} %get-tuple-element.20, f32[2,5,512,512]{2,3,1,0:T(8,128)S(1)} %bitcast.79, pred[2,512]{1,0:T(4,128)(4,1)S(1)} %get-tuple-element.19, f32[2,5,512]{2,1,0:T(8,128)S(1)} %neg.9, ...), kind=kLoop, calls=%fused_computation.62 | loop fusion | flops 26209280 | bytes 31540224 | tf_op jit(solution)/shard_map/vmap(transpose(jvp()))/reduce_sum | solution.py:28
  189.9 2.3 copy-done.1
  192.2 1.0 fusion.18
  193.2 4.3 fusion.16
  197.5 0.0 reduce-scatter.5.cloned.1.call-update
  197.5 0.0 reduce-scatter.3.cloned.1.call-start
  197.5 0.7 copy.18
  198.2 0.1 copy.33
  198.3 6.2 %convolution_convert_fusion = bf16[1024,2560]{0,1:T(8,128)(2,1)} fusion(bf16[320,2560]{0,1:T(8,128)(2,1)} %all-gather.3.cloned.1.call-done, bf16[1024,320]{0,1:T(8,128)(2,1)S(1)} %bitcast.99), kind=kOutput, calls=%fused_computation.15 | convolution fusion | flops 1680343040 | bytes 7536640 | tf_op jit(solution)/shard_map/dot_general | solution.py:58
  204.5 0.0 reduce-scatter.3.cloned.1.call-update
  204.5 4.3 convolution_convert_fusion.2
  208.9 7.2 %fusion.20 = bf16[2,5,512,64]{2,3,1,0:T(8,128)(2,1)} fusion(bf16[2,512,5,64]{1,3,2,0:T(8,128)(2,1)S(1)} %bitcast.93, f32[2,5,512,512]{2,3,1,0:T(8,128)} %get-tuple-element.10, pred[2,5,512,512]{2,3,1,0:T(32,128)(4,1)} %get-tuple-element.12, f32[2,5,512]{2,1,0:T(8,128)S(1)} %negate_divide_fusion, pred[2,512]{1,0:T(4,128)(4,1)S(1)} %get-tuple-element.19), kind=kOutput, calls=%fused_computation.36 | convolution fusion | flops 346357760 | bytes 14439424 | tf_op jit(solution)/shard_map/vmap(transpose(jvp(qhd,khd->hqk)))/dot_general | solution.py:21
  216.1 0.0 copy-start.8
  216.1 4.6 %fusion.19 = bf16[2,5,512,64]{2,3,1,0:T(8,128)(2,1)S(1)} fusion(bf16[2,512,5,64]{1,3,2,0:T(8,128)(2,1)S(1)} %bitcast.91, f32[2,5,512,512]{2,3,1,0:T(8,128)S(1)} %bitcast.81, pred[2,5,512,512]{2,3,1,0:T(32,128)(4,1)} %get-tuple-element.12, f32[2,5,512]{2,1,0:T(8,128)S(1)} %negate_divide_fusion, pred[2,512]{1,0:T(4,128)(4,1)S(1)} %get-tuple-element.19), kind=kOutput, calls=%fused_computation.35 | convolution fusion | flops 346357760 | bytes 14439424 | tf_op jit(solution)/shard_map/vmap(transpose(jvp(qhd,khd->hqk)))/dot_general | solution.py:21
  220.7 0.2 add_bitcast_fusion
  220.9 1.0 slice_bitcast_fusion.1
  221.9 3.9 collective-permute-start.2
  225.7 43.2 %collective-permute-done.2 = bf16[3,512,320]{1,2,0:T(8,128)(2,1)S(1)} collective-permute-done((bf16[3,512,320]{1,2,0:T(8,128)(2,1)}, bf16[3,512,320]{1,2,0:T(8,128)(2,1)S(1)}, u32[]{:S(2)}, u32[]{:S(2)}) %collective-permute-start.2) | collective-permute-done | bytes 983072 | tf_op jit(solution)/shard_map/ppermute | solution.py:11
  269.0 1.0 fusion.24
  270.0 58.0 %reduce-scatter.5.cloned.1.call-done = bf16[320,80]{0,1:T(8,128)(2,1)} async-done(((bf16[320,2560]{0,1:T(8,128)(2,1)}), bf16[320,80]{0,1:T(8,128)(2,1)}) %reduce-scatter.5.cloned.1.call-update) | async-done | bytes 51216 | tf_op jit(solution)/shard_map/reduce_scatter | solution.py:72
  328.0 1.5 convert_element_type.92
  329.5 105.2 %reduce-scatter.3.cloned.1.call-done = bf16[1024,320]{0,1:T(8,128)(2,1)} async-done(((bf16[1024,2560]{0,1:T(8,128)(2,1)}), bf16[1024,320]{0,1:T(8,128)(2,1)}) %reduce-scatter.3.cloned.1.call-update) | async-done | bytes 655376 | tf_op jit(solution)/shard_map/reduce_scatter | solution.py:59
  434.7 2.0 copy.44
  (34 shorter events, 0.1 us)
Async XLA Ops:
  7.2 91.6 %all-gather.5.cloned.1.call-start = ((), (), s32[]{:S(2)}) async-start(), calls=%async_computation.4 | async-start | bytes 5898240 | tf_op jit(solution)/shard_map/all_gather | solution.py:63
  7.9 156.0 %all-gather.3.cloned.1.call-start = ((), (), s32[]{:S(2)}) async-start(), calls=%async_computation.2 | async-start | bytes 2027520 | tf_op jit(solution)/shard_map/all_gather | solution.py:57
  8.6 319.3 %reduce-scatter.5.cloned.1.call-start = ((), (), s32[]{:S(2)}) async-start(), calls=%async_computation.5 | async-start | bytes 2027520 | tf_op jit(solution)/shard_map/reduce_scatter | solution.py:72
  8.7 33.9 %collective-permute-start = (bf16[3,512,320]{1,2,0:T(8,128)(2,1)}, bf16[3,512,320]{1,2,0:T(8,128)(2,1)S(1)}, u32[]{:S(2)}, u32[]{:S(2)}) collective-permute-start(bf16[3,512,320]{1,2,0:T(8,128)(2,1)} %param.5), channel_id=1, source_target_pairs={{0,128},{8,136},{16,144},{24,152},{32,160},{40,168},{48,176},{56,1... | collective-permute-start | bytes 2949128 | tf_op jit(solution)/shard_map/ppermute | solution.py:11
  17.9 24.5 %collective-permute-start.1 = (s32[2]{0:T(128)S(1)}, s32[2]{0:T(128)S(1)}, u32[]{:S(2)}, u32[]{:S(2)}) collective-permute-start(s32[2]{0:T(128)S(1)} %pad_add_fusion), channel_id=1, source_target_pairs={{0,128},{8,136},{16,144},{24,152},{32,160},{40,168},{48,176},{56,1... | collective-permute-start | bytes 32 | tf_op jit(solution)/shard_map/ppermute | solution.py:11
  43.9 2.6 copy-start.4
  43.9 2.6 copy-start.6
  43.9 128.6 %copy-start.2 = (bf16[1,2,512,320]{2,3,0,1:T(8,128)(2,1)}, bf16[1,2,512,320]{2,3,0,1:T(8,128)(2,1)S(1)}, u32[]{:S(2)}) copy-start(bf16[1,2,512,320]{2,3,0,1:T(8,128)(2,1)S(1)} %get-tuple-element.16) | copy-start | bytes 1966084
  46.5 4.0 copy-start
  170.0 23.1 %slice-start.6 = ((s8[5242880]{0:T(1024)(128)(4,1)}), s8[1048576]{0:T(1024)(128)(4,1)S(1)}, s32[]{:S(2)}) async-start(s8[5242880]{0:T(1024)(128)(4,1)} %bitcast.82), calls=%async_computation.12 | async-start | bytes 2097152
  172.5 11.0 %slice-start = ((s8[10485760]{0:T(1024)(128)(4,1)}), s8[4194304]{0:T(1024)(128)(4,1)S(1)}, s32[]{:S(2)}) async-start(s8[10485760]{0:T(1024)(128)(4,1)} %bitcast.78), calls=%async_computation.6 | async-start | bytes 8388608
  172.6 11.0 %slice-start.1 = ((s8[10485760]{0:T(1024)(128)(4,1)}), s8[4194304]{0:T(1024)(128)(4,1)S(1)}, s32[]{:S(2)}) async-start(s8[10485760]{0:T(1024)(128)(4,1)} %bitcast.78), calls=%async_computation.7 | async-start | bytes 8388608
  172.6 11.0 %slice-start.2 = ((s8[10485760]{0:T(1024)(128)(4,1)}), s8[2097152]{0:T(1024)(128)(4,1)S(1)}, s32[]{:S(2)}) async-start(s8[10485760]{0:T(1024)(128)(4,1)} %bitcast.78), calls=%async_computation.8 | async-start | bytes 4194304
  172.6 20.6 %slice-start.7 = ((s8[5242880]{0:T(1024)(128)(4,1)}), s8[4194304]{0:T(1024)(128)(4,1)S(1)}, s32[]{:S(2)}) async-start(s8[5242880]{0:T(1024)(128)(4,1)} %bitcast.82), calls=%async_computation.13 | async-start | bytes 8388608
  183.6 8.6 %copy-start.3 = (bf16[1,2,512,320]{2,3,0,1:T(8,128)(2,1)S(1)}, bf16[1,2,512,320]{2,3,0,1:T(8,128)(2,1)}, u32[]{:S(2)}) copy-start(bf16[1,2,512,320]{2,3,0,1:T(8,128)(2,1)} %copy-done.2) | copy-start | bytes 1966084
  189.9 2.3 copy-start.1
  197.5 237.2 %reduce-scatter.3.cloned.1.call-start = ((), (), s32[]{:S(2)}) async-start(), calls=%async_computation.3 | async-start | bytes 5898240 | tf_op jit(solution)/shard_map/reduce_scatter | solution.py:59
  204.5 4.4 copy-start.7
  204.5 11.5 %slice-start.3 = ((s8[10485760]{0:T(1024)(128)(4,1)}), s8[4194304]{0:T(1024)(128)(4,1)S(1)}, s32[]{:S(2)}) async-start(s8[10485760]{0:T(1024)(128)(4,1)} %bitcast.80), calls=%async_computation.9 | async-start | bytes 8388608
  208.9 7.2 %slice-start.4 = ((s8[10485760]{0:T(1024)(128)(4,1)}), s8[4194304]{0:T(1024)(128)(4,1)S(1)}, s32[]{:S(2)}) async-start(s8[10485760]{0:T(1024)(128)(4,1)} %bitcast.80), calls=%async_computation.10 | async-start | bytes 8388608
  208.9 7.2 %slice-start.5 = ((s8[10485760]{0:T(1024)(128)(4,1)}), s8[2097152]{0:T(1024)(128)(4,1)S(1)}, s32[]{:S(2)}) async-start(s8[10485760]{0:T(1024)(128)(4,1)} %bitcast.80), calls=%async_computation.11 | async-start | bytes 4194304
  208.9 7.2 %copy-start.5 = (bf16[1,2,512,320]{2,3,0,1:T(8,128)(2,1)S(1)}, bf16[1,2,512,320]{2,3,0,1:T(8,128)(2,1)}, u32[]{:S(2)}) copy-start(bf16[1,2,512,320]{2,3,0,1:T(8,128)(2,1)} %copy-done.4) | copy-start | bytes 1966084
  216.1 4.6 %copy-start.8 = (bf16[2,5,512,64]{2,3,1,0:T(8,128)(2,1)S(1)}, bf16[2,5,512,64]{2,3,1,0:T(8,128)(2,1)}, u32[]{:S(2)}) copy-start(bf16[2,5,512,64]{2,3,1,0:T(8,128)(2,1)} %fusion.20) | copy-start | bytes 1966084
  221.9 47.1 %collective-permute-start.2 = (bf16[3,512,320]{1,2,0:T(8,128)(2,1)}, bf16[3,512,320]{1,2,0:T(8,128)(2,1)S(1)}, u32[]{:S(2)}, u32[]{:S(2)}) collective-permute-start(bf16[3,512,320]{1,2,0:T(8,128)(2,1)} %slice_bitcast_fusion.1), channel_id=1, source_target_pairs={{0,128},{8,136},{16,144},{24,152},{32,160},{40,168},{48,176},{56,1... | collective-permute-start | bytes 2949128 | tf_op jit(solution)/shard_map/ppermute | solution.py:11
Sparse Core Ops, SparseCore 0:
  10.6 88.1 all-gather.4
  100.6 63.3 all-gather.2
  197.6 130.3 reduce-scatter.4
  332.0 102.6 reduce-scatter.2
where the time goes:
time: 444 us; the launch traced here: 443 us
  waiting for transfers between devices  338 us (76%)
  matrix products  47 us (11%)
  local copies, waits for them, and re-layouts  18.1 us (4%)
  between operations  15.4 us (3%)
  other arithmetic  13.1 us (3%)
  starting transfers between devices  11.9 us (3%)
    reduce_scatter x1, waiting for transfers between devices, shards(): lax.psum_scatter(partial_value.astype(jnp.bfloat16), 'tensor', scatter_di...  105 us
    ppermute x3, waiting for transfers between devices, shifted(): lax.ppermute(shard, axis, [(i, (i + by) % peers) for i in range(peers)])  67.7 us
    reduce_scatter x1, waiting for transfers between devices, shards(): lax.psum_scatter(weight_term.astype(jnp.bfloat16), 'dp', scatter_dimensio...  58 us
    all_gather x1, waiting for transfers between devices, shards(): whole_weight = lax.all_gather(out_weight, 'dp', axis=1, tiled=True)  57.2 us
    all_gather x1, waiting for transfers between devices, shards(): lax.all_gather(out_cotangent, 'tensor', axis=2, tiled=True)  48.2 us
    dot_general x3, matrix products, attend(): jnp.einsum('hqk,khd->qhd', weights, values, preferred_element_type=jnp.fl...  16.2 us
    dot_general x3, matrix products, attend(): jnp.einsum('qhd,khd->hqk', queries, key_rows, preferred_element_type=jnp....  14.3 us
    ppermute x3, starting transfers between devices, shifted(): lax.ppermute(shard, axis, [(i, (i + by) % peers) for i in range(peers)])  11.7 us
  transfers between devices with their start and end apart: 7, of which 6 were waited for; matrix products, arithmetic and copies ran while one was open for 9% of the time, Pallas kernels for 0%

commit v1 on v0

--- a/solution.py
+++ b/solution.py
@@ -60,7 +60,9 @@
         partial_value.astype(jnp.bfloat16), "tensor", scatter_dimension=1, tiled=True
     )
     layer_out = summed.reshape(home_tiles + 1, length, -1)
-    full_cot = lax.all_gather(out_cotangent, "tensor", axis=2, tiled=True).reshape(row_count, -1)
+    full_cot = jnp.concatenate(
+        lax.all_to_all(jnp.stack([out_cotangent] * lax.axis_size("tensor")), "tensor", 0, 0), axis=2
+    ).reshape(row_count, -1)
     contract_cols = (((1,), (1,)), ((), ()))
     grad_context = lax.dot_general(
         full_cot, whole_weight, contract_cols, preferred_element_type=jnp.float32

time: 444 us -> 403 us (0.908)
  waiting for transfers between devices: 338 us -> 286 us
  starting transfers between devices: 11.9 us -> 18.7 us
  local copies, waits for them, and re-layouts: 18.1 us -> 23.5 us
    all_gather x1 -> x0, waiting for transfers between devices: 48.2 us -> none  [shards(): lax.all_gather(out_cotangent, 'tensor', axis=2, tiled=True)]
    all_gather x1, waiting for transfers between devices: 57.2 us -> 18.6 us  [shards(): whole_weight = lax.all_gather(out_weight, 'dp', axis=1, tiled=True)]
    all_to_all x0 -> x1, waiting for transfers between devices: none -> 31.5 us  [shards(): lax.all_to_all(jnp.stack([out_cotangent] * lax.axis_size('tensor')), 'ten...]
    reduce_scatter x1, waiting for transfers between devices: 58 us -> 69.1 us  [shards(): lax.psum_scatter(weight_term.astype(jnp.bfloat16), 'dp', scatter_dimensio...]
    unnamed x35, local copies, waits for them, and re-layouts: 3.98 us -> 12.3 us
    all_gather x1 -> x0, local copies, waits for them, and re-layouts: 7.98 us -> none  [shards(): lax.all_gather(out_cotangent, 'tensor', axis=2, tiled=True)]
    all_to_all x0 -> x1, starting transfers between devices: none -> 7.6 us  [shards(): lax.all_to_all(jnp.stack([out_cotangent] * lax.axis_size('tensor')), 'ten...]
    reduce_scatter x1, waiting for transfers between devices: 105 us -> 98.9 us  [shards(): lax.psum_scatter(partial_value.astype(jnp.bfloat16), 'tensor', scatter_di...]
where the time goes in v1:
time: 403 us
  waiting for transfers between devices  286 us (71%)
  matrix products  46.8 us (12%)
  local copies, waits for them, and re-layouts  23.5 us (6%)
  starting transfers between devices  18.7 us (5%)
  between operations  15.3 us (4%)
  other arithmetic  12.2 us (3%)
    reduce_scatter x1, waiting for transfers between devices, shards(): lax.psum_scatter(partial_value.astype(jnp.bfloat16), 'tensor', scatter_di...  98.9 us
    reduce_scatter x1, waiting for transfers between devices, shards(): lax.psum_scatter(weight_term.astype(jnp.bfloat16), 'dp', scatter_dimensio...  69.1 us
    ppermute x3, waiting for transfers between devices, shifted(): lax.ppermute(shard, axis, [(i, (i + by) % peers) for i in range(peers)])  67.2 us
    all_to_all x1, waiting for transfers between devices, shards(): lax.all_to_all(jnp.stack([out_cotangent] * lax.axis_size('tensor')), 'ten...  31.5 us
    all_gather x1, waiting for transfers between devices, shards(): whole_weight = lax.all_gather(out_weight, 'dp', axis=1, tiled=True)  18.6 us
    dot_general x3, matrix products, attend(): jnp.einsum('hqk,khd->qhd', weights, values, preferred_element_type=jnp.fl...  16.2 us
    dot_general x3, matrix products, attend(): jnp.einsum('qhd,khd->hqk', queries, key_rows, preferred_element_type=jnp....  14.3 us
    unnamed x35, local copies, waits for them, and re-layouts  12.3 us
  transfers between devices with their start and end apart: 7, of which 6 were waited for; matrix products, arithmetic and copies ran while one was open for 9% of the time, Pallas kernels for 0%

profile of v1, /device:TPU:1, one launch (start us, length us, event | category | flops | bytes accessed | tf_op | source)
XLA Modules:
  0.0 402.5 jit_solution(3315725192377750830)
XLA Ops:
  7.2 1.8 copy.20
  8.9 5.0 %stack.8 = bf16[8,2,512,320]{2,1,3,0:T(2,128)(2,1)} broadcast(bf16[2,512,320]{1,0,2:T(2,128)(2,1)S(1)} %copy.20), dimensions={1,2,3} | broadcast | bytes 5898240 | tf_op jit(solution)/shard_map/stack | solution.py:64
  14.0 7.6 %all-to-all-start = ((bf16[8,2,512,320]{2,1,3,0:T(2,128)(2,1)}), bf16[8,2,512,320]{2,1,3,0:T(2,128)(2,1)}, u32[]{:S(2)}, u32[]{:S(2)}) async-start(bf16[8,2,512,320]{2,1,3,0:T(2,128)(2,1)} %stack.8), calls=%async_computation.1 | async-start | bytes 10485760 | tf_op jit(solution)/shard_map/all_to_all | solution.py:64
  21.6 0.0 all-gather.2.cloned.1.call-start
  21.6 0.7 all-gather.2.cloned.1.call-update
  22.3 0.0 reduce-scatter.5.cloned.1.call-start
  22.4 7.0 %collective-permute-start = (bf16[3,512,320]{1,2,0:T(8,128)(2,1)S(1)}, bf16[3,512,320]{1,2,0:T(8,128)(2,1)S(1)}, u32[]{:S(2)}, u32[]{:S(2)}) collective-permute-start(bf16[3,512,320]{1,2,0:T(8,128)(2,1)S(1)} %copy-done.6), channel_id=1, source_target_pairs={{0,128},{8,136},{16,144},{24,152},{32,160},{40,168},{48,176},{56,1... | collective-permute-start | bytes 2949128 | tf_op jit(solution)/shard_map/ppermute | solution.py:11
  30.7 0.1 pad_add_fusion
  30.7 0.2 collective-permute-start.1
  31.0 25.2 %collective-permute-done.1 = s32[2]{0:T(128)S(1)} collective-permute-done((s32[2]{0:T(128)S(1)}, s32[2]{0:T(128)S(1)}, u32[]{:S(2)}, u32[]{:S(2)}) %collective-permute-start.1) | collective-permute-done | bytes 40 | tf_op jit(solution)/shard_map/ppermute | solution.py:11
  56.2 0.1 pad_add_fusion.1
  56.3 0.1 fusion.33
  56.4 0.2 pad_maximum_fusion
  56.5 0.0 copy-start.2
  56.5 0.0 copy-start.4
  56.5 2.5 fusion.5
  59.1 2.4 fusion.16
  61.6 1.5 copy-done
  63.1 31.5 %all-to-all-done = bf16[8,2,512,320]{2,1,3,0:T(2,128)(2,1)} async-done(((bf16[8,2,512,320]{2,1,3,0:T(2,128)(2,1)}), bf16[8,2,512,320]{2,1,3,0:T(2,128)(2,1)}, u32[]{:S(2)}, u32[]{:S(2)}) %all-to-all-start) | async-done | bytes 5242912 | tf_op jit(solution)/shard_map/all_to_all | solution.py:64
  94.6 6.6 %copy.35 = bf16[320,8,2,512]{3,1,2,0:T(8,128)(2,1)} copy(bf16[320,8,2,512]{3,2,1,0:T(2,128)(2,1)} %bitcast.39) | data formatting | bytes 10485760
  101.2 18.6 %all-gather.2.cloned.1.call-done = bf16[320,2560]{0,1:T(8,128)(2,1)} async-done(((bf16[320,80]{0,1:T(8,128)(2,1)}), bf16[320,2560]{0,1:T(8,128)(2,1)}) %all-gather.2.cloned.1.call-update) | async-done | bytes 1638416 | tf_op jit(solution)/shard_map/all_gather | solution.py:57
  119.8 6.1 %fusion.20 = f32[1024,320]{0,1:T(8,128)} fusion(bf16[1024,2560]{0,1:T(8,128)(2,1)} %bitcast.82, bf16[320,2560]{0,1:T(8,128)(2,1)} %all-gather.2.cloned.1.call-done), kind=kOutput, calls=%fused_computation.38 | convolution fusion | flops 1678376960 | bytes 8192000 | tf_op jit(solution)/shard_map/dot_general | solution.py:67
  125.9 2.5 reshape.95
  128.4 10.9 %convert_reduce_fusion = (f32[2,5,512]{2,1,0:T(8,128)S(1)}, pred[2,5,512,512]{2,3,1,0:T(32,128)(4,1)}, f32[2,5,512]{2,1,0:T(8,128)S(1)}, bf16[2,5,512,512]{2,3,1,0:T(8,128)(2,1)S(1)}) fusion(f32[2,5,512]{2,1,0:T(8,128)S(1)} %get-tuple-element.20, f32[2,5,512,512]{2,3,1,0:T(8,128)} %copy-done, pred[2,512]{1,0:T(4,128)(4,1)S(1)} %get-tuple-element.19, ...), kind=kOutput, calls=%fused_computation.7 | convolution fusion | flops 364697600 | bytes 20403200 | tf_op jit(solution)/shard_map/vmap(transpose(jvp(hqk,khd->qhd)))/dot_general | solution.py:30
  139.3 6.6 %fusion.34 = (f32[2,5,512]{2,1,0:T(8,128)S(1)}, f32[2,5,512,512]{2,3,1,0:T(8,128)}, bf16[2,5,512,512]{2,3,1,0:T(8,128)(2,1)S(1)}) fusion(f32[2,5,512]{2,1,0:T(8,128)S(1)} %get-tuple-element.20, f32[2,5,512,512]{2,3,1,0:T(8,128)S(1)} %bitcast.79, pred[2,512]{1,0:T(4,128)(4,1)S(1)} %get-tuple-element.19, f32[2,5,512]{2,1,0:T(8,128)S(1)} %neg.9, ...), kind=kLoop, calls=%fused_computation.62 | loop fusion | flops 26209280 | bytes 31540224 | tf_op jit(solution)/shard_map/vmap(transpose(jvp()))/reduce_sum | solution.py:28
  145.9 2.2 copy-done.1
  148.1 1.0 fusion.23
  149.1 0.7 copy.19
  149.8 0.1 copy.34
  149.9 4.1 %convolution_convert_fusion.1 = bf16[320,2560]{0,1:T(8,128)(2,1)} fusion(bf16[1024,320]{0,1:T(8,128)(2,1)S(1)} %bitcast.97, bf16[1024,2560]{0,1:T(8,128)(2,1)S(1)} %bitcast.85), kind=kOutput, calls=%fused_computation.24 | convolution fusion | flops 1678540800 | bytes 7536640 | tf_op jit(solution)/shard_map/dot_general | solution.py:71
  154.0 0.0 reduce-scatter.5.cloned.1.call-update
  154.0 0.0 reduce-scatter.3.cloned.1.call-start
  154.1 6.1 %convolution_convert_fusion = bf16[1024,2560]{0,1:T(8,128)(2,1)} fusion(bf16[320,2560]{0,1:T(8,128)(2,1)} %all-gather.2.cloned.1.call-done, bf16[1024,320]{0,1:T(8,128)(2,1)S(1)} %bitcast.98), kind=kOutput, calls=%fused_computation.15 | convolution fusion | flops 1680343040 | bytes 7536640 | tf_op jit(solution)/shard_map/dot_general | solution.py:58
  160.2 0.0 reduce-scatter.3.cloned.1.call-update
  160.3 4.3 %convolution_convert_fusion.3 = bf16[2,5,64,512]{3,2,1,0:T(8,128)(2,1)S(1)} fusion(bf16[2,5,512,512]{2,3,1,0:T(8,128)(2,1)} %copy-done.1, f32[2,512,5,64]{1,0,3,2:T(2,128)S(1)} %reshape.95, f32[2,512]{1,0:T(2,128)S(1)} %get-tuple-element.18), kind=kOutput, calls=%fused_computation.36 | convolution fusion | flops 336199680 | bytes 7213056 | tf_op jit(solution)/shard_map/vmap(transpose(jvp(hqk,khd->qhd)))/dot_general | solution.py:30
  164.6 0.0 copy-start.3
  164.7 7.2 %fusion.19 = bf16[2,5,512,64]{2,3,1,0:T(8,128)(2,1)} fusion(bf16[2,512,5,64]{1,3,2,0:T(8,128)(2,1)S(1)} %bitcast.92, f32[2,5,512,512]{2,3,1,0:T(8,128)} %get-tuple-element.10, pred[2,5,512,512]{2,3,1,0:T(32,128)(4,1)} %get-tuple-element.12, f32[2,5,512]{2,1,0:T(8,128)S(1)} %negate_divide_fusion, pred[2,512]{1,0:T(4,128)(4,1)S(1)} %get-tuple-element.19), kind=kOutput, calls=%fused_computation.35 | convolution fusion | flops 346357760 | bytes 14439424 | tf_op jit(solution)/shard_map/vmap(transpose(jvp(qhd,khd->hqk)))/dot_general | solution.py:21
  171.9 0.0 copy-start.7
  171.9 4.6 %fusion.18 = bf16[2,5,512,64]{2,3,1,0:T(8,128)(2,1)S(1)} fusion(bf16[2,512,5,64]{1,3,2,0:T(8,128)(2,1)S(1)} %bitcast.90, f32[2,5,512,512]{2,3,1,0:T(8,128)S(1)} %bitcast.81, pred[2,5,512,512]{2,3,1,0:T(32,128)(4,1)} %get-tuple-element.12, f32[2,5,512]{2,1,0:T(8,128)S(1)} %negate_divide_fusion, pred[2,512]{1,0:T(4,128)(4,1)S(1)} %get-tuple-element.19), kind=kOutput, calls=%fused_computation.34 | convolution fusion | flops 346357760 | bytes 14439424 | tf_op jit(solution)/shard_map/vmap(transpose(jvp(qhd,khd->hqk)))/dot_general | solution.py:21
  176.5 0.2 add_bitcast_fusion
  176.7 1.0 slice_bitcast_fusion.1
  177.7 3.8 collective-permute-start.2
  181.5 42.0 %collective-permute-done.2 = bf16[3,512,320]{1,2,0:T(8,128)(2,1)S(1)} collective-permute-done((bf16[3,512,320]{1,2,0:T(8,128)(2,1)}, bf16[3,512,320]{1,2,0:T(8,128)(2,1)S(1)}, u32[]{:S(2)}, u32[]{:S(2)}) %collective-permute-start.2) | collective-permute-done | bytes 983072 | tf_op jit(solution)/shard_map/ppermute | solution.py:11
  223.5 1.0 fusion.24
  224.5 69.1 %reduce-scatter.5.cloned.1.call-done = bf16[320,80]{0,1:T(8,128)(2,1)} async-done(((bf16[320,2560]{0,1:T(8,128)(2,1)}), bf16[320,80]{0,1:T(8,128)(2,1)}) %reduce-scatter.5.cloned.1.call-update) | async-done | bytes 51216 | tf_op jit(solution)/shard_map/reduce_scatter | solution.py:74
  293.6 1.5 convert_element_type.89
  295.1 98.9 %reduce-scatter.3.cloned.1.call-done = bf16[1024,320]{0,1:T(8,128)(2,1)} async-done(((bf16[1024,2560]{0,1:T(8,128)(2,1)}), bf16[1024,320]{0,1:T(8,128)(2,1)}) %reduce-scatter.3.cloned.1.call-update) | async-done | bytes 655376 | tf_op jit(solution)/shard_map/reduce_scatter | solution.py:59
  394.0 2.0 copy.46
  (33 shorter events, 0.1 us)
Async XLA Ops:
  14.0 8.4 %copy-start.6 = (bf16[3,512,320]{1,2,0:T(8,128)(2,1)S(1)}, bf16[3,512,320]{1,2,0:T(8,128)(2,1)}, u32[]{:S(2)}) copy-start(bf16[3,512,320]{1,2,0:T(8,128)(2,1)} %param.5) | copy-start | bytes 2949124
  14.0 80.6 %all-to-all-start = ((bf16[8,2,512,320]{2,1,3,0:T(2,128)(2,1)}), bf16[8,2,512,320]{2,1,3,0:T(2,128)(2,1)}, u32[]{:S(2)}, u32[]{:S(2)}) async-start(bf16[8,2,512,320]{2,1,3,0:T(2,128)(2,1)} %stack.8), calls=%async_computation.1 | async-start | bytes 10485760 | tf_op jit(solution)/shard_map/all_to_all | solution.py:64
  21.6 98.2 %all-gather.2.cloned.1.call-start = ((), (), s32[]{:S(2)}) async-start(), calls=%async_computation.3 | async-start | bytes 2027520 | tf_op jit(solution)/shard_map/all_gather | solution.py:57
  22.3 271.3 %reduce-scatter.5.cloned.1.call-start = ((), (), s32[]{:S(2)}) async-start(), calls=%async_computation.5 | async-start | bytes 2027520 | tf_op jit(solution)/shard_map/reduce_scatter | solution.py:74
  22.4 34.0 %collective-permute-start = (bf16[3,512,320]{1,2,0:T(8,128)(2,1)S(1)}, bf16[3,512,320]{1,2,0:T(8,128)(2,1)S(1)}, u32[]{:S(2)}, u32[]{:S(2)}) collective-permute-start(bf16[3,512,320]{1,2,0:T(8,128)(2,1)S(1)} %copy-done.6), channel_id=1, source_target_pairs={{0,128},{8,136},{16,144},{24,152},{32,160},{40,168},{48,176},{56,1... | collective-permute-start | bytes 2949128 | tf_op jit(solution)/shard_map/ppermute | solution.py:11
  30.7 25.4 %collective-permute-start.1 = (s32[2]{0:T(128)S(1)}, s32[2]{0:T(128)S(1)}, u32[]{:S(2)}, u32[]{:S(2)}) collective-permute-start(s32[2]{0:T(128)S(1)} %pad_add_fusion), channel_id=1, source_target_pairs={{0,128},{8,136},{16,144},{24,152},{32,160},{40,168},{48,176},{56,1... | collective-permute-start | bytes 32 | tf_op jit(solution)/shard_map/ppermute | solution.py:11
  56.5 2.6 copy-start.2
  56.5 2.6 copy-start.4
  59.1 4.0 copy-start
  125.9 24.0 %slice-start.6 = ((s8[5242880]{0:T(1024)(128)(4,1)}), s8[1048576]{0:T(1024)(128)(4,1)S(1)}, s32[]{:S(2)}) async-start(s8[5242880]{0:T(1024)(128)(4,1)} %bitcast.83), calls=%async_computation.12 | async-start | bytes 2097152
  128.4 10.9 %slice-start = ((s8[10485760]{0:T(1024)(128)(4,1)}), s8[4194304]{0:T(1024)(128)(4,1)S(1)}, s32[]{:S(2)}) async-start(s8[10485760]{0:T(1024)(128)(4,1)} %bitcast.78), calls=%async_computation.6 | async-start | bytes 8388608
  128.4 10.9 %slice-start.1 = ((s8[10485760]{0:T(1024)(128)(4,1)}), s8[4194304]{0:T(1024)(128)(4,1)S(1)}, s32[]{:S(2)}) async-start(s8[10485760]{0:T(1024)(128)(4,1)} %bitcast.78), calls=%async_computation.7 | async-start | bytes 8388608
  128.4 10.9 %slice-start.2 = ((s8[10485760]{0:T(1024)(128)(4,1)}), s8[2097152]{0:T(1024)(128)(4,1)S(1)}, s32[]{:S(2)}) async-start(s8[10485760]{0:T(1024)(128)(4,1)} %bitcast.78), calls=%async_computation.8 | async-start | bytes 4194304
  128.4 21.5 %slice-start.7 = ((s8[5242880]{0:T(1024)(128)(4,1)}), s8[4194304]{0:T(1024)(128)(4,1)S(1)}, s32[]{:S(2)}) async-start(s8[5242880]{0:T(1024)(128)(4,1)} %bitcast.83), calls=%async_computation.13 | async-start | bytes 8388608
  145.9 2.2 copy-start.1
  154.0 240.0 %reduce-scatter.3.cloned.1.call-start = ((), (), s32[]{:S(2)}) async-start(), calls=%async_computation.4 | async-start | bytes 5898240 | tf_op jit(solution)/shard_map/reduce_scatter | solution.py:59
  160.2 4.4 %copy-start.5 = (bf16[1,2,512,320]{2,3,0,1:T(8,128)(2,1)S(1)}, bf16[1,2,512,320]{2,3,0,1:T(8,128)(2,1)}, u32[]{:S(2)}) copy-start(bf16[1,2,512,320]{2,3,0,1:T(8,128)(2,1)} %copy-done.4) | copy-start | bytes 1966084
  160.3 11.6 %slice-start.3 = ((s8[10485760]{0:T(1024)(128)(4,1)}), s8[4194304]{0:T(1024)(128)(4,1)S(1)}, s32[]{:S(2)}) async-start(s8[10485760]{0:T(1024)(128)(4,1)} %bitcast.80), calls=%async_computation.9 | async-start | bytes 8388608
  164.6 7.2 %slice-start.4 = ((s8[10485760]{0:T(1024)(128)(4,1)}), s8[4194304]{0:T(1024)(128)(4,1)S(1)}, s32[]{:S(2)}) async-start(s8[10485760]{0:T(1024)(128)(4,1)} %bitcast.80), calls=%async_computation.10 | async-start | bytes 8388608
  164.6 7.2 %slice-start.5 = ((s8[10485760]{0:T(1024)(128)(4,1)}), s8[2097152]{0:T(1024)(128)(4,1)S(1)}, s32[]{:S(2)}) async-start(s8[10485760]{0:T(1024)(128)(4,1)} %bitcast.80), calls=%async_computation.11 | async-start | bytes 4194304
  164.6 7.2 %copy-start.3 = (bf16[1,2,512,320]{2,3,0,1:T(8,128)(2,1)S(1)}, bf16[1,2,512,320]{2,3,0,1:T(8,128)(2,1)}, u32[]{:S(2)}) copy-start(bf16[1,2,512,320]{2,3,0,1:T(8,128)(2,1)} %copy-done.2) | copy-start | bytes 1966084
  171.9 4.6 %copy-start.7 = (bf16[2,5,512,64]{2,3,1,0:T(8,128)(2,1)S(1)}, bf16[2,5,512,64]{2,3,1,0:T(8,128)(2,1)}, u32[]{:S(2)}) copy-start(bf16[2,5,512,64]{2,3,1,0:T(8,128)(2,1)} %fusion.19) | copy-start | bytes 1966084
  177.7 45.8 %collective-permute-start.2 = (bf16[3,512,320]{1,2,0:T(8,128)(2,1)}, bf16[3,512,320]{1,2,0:T(8,128)(2,1)S(1)}, u32[]{:S(2)}, u32[]{:S(2)}) collective-permute-start(bf16[3,512,320]{1,2,0:T(8,128)(2,1)} %slice_bitcast_fusion.1), channel_id=1, source_target_pairs={{0,128},{8,136},{16,144},{24,152},{32,160},{40,168},{48,176},{56,1... | collective-permute-start | bytes 2949128 | tf_op jit(solution)/shard_map/ppermute | solution.py:11
Sparse Core Ops, SparseCore 0:
  24.2 95.5 all-gather.1
  154.2 139.3 reduce-scatter.4
  297.8 96.1 reduce-scatter.2
